TPU v7x, 256 devices: a whole 4x4x8 slice. The times are simulated.
256 devices in a mesh: batch: 16 (over z, core), proto: 16 (over x, y).
Axes of the slice: x: 4, y: 4, z: 8, core: 2. Of those that a mesh axis runs over, the one named last changes fastest.
Arguments:
- slow_embed: bfloat16 [16384, 256], P('batch'), may hold values from -1 to 1
- fast_embed: bfloat16 [16384, 256], P('batch'), may hold values from -1 to 1
- prototypes: float32 [32768, 256], P('proto'), may hold values from -1 to 1
Outputs:
- proto_grad: float32 [32768, 256], P('proto')
- slow_grad: float32 [16384, 256], P('batch')
- fast_grad: float32 [16384, 256], P('batch')
All inputs are finite; a program needn't handle non-finite values.
Results may differ from a plain program's by a relative error of at most 0.0005.
The roundings to bfloat16 on the way count: a program that leaves them out, or rounds other values in their place, can miss the bound.
Values sent between devices are 32-bit elements; how exact they have to be, the bound alone decides.
A program may use at most 128 MiB of HBM per device.

v0:
```python
import jax
import jax.numpy as jnp
from jax import lax
from jax.sharding import PartitionSpec as P

ITERS = 3
CODE_EPS = 0.05
TEMPER = 0.1
NORM_EPS = 1e-06


def normalize(raw_rows):
    lengths = jnp.sqrt(jnp.sum(raw_rows * raw_rows, axis=-1, keepdims=True) + 1e-12)
    return (raw_rows / lengths, lengths)


def project_back(grad_unit, unit_vec, lengths):
    along = jnp.sum(unit_vec * grad_unit, axis=-1, keepdims=True)
    return (grad_unit - unit_vec * along) / lengths


def row_total(row_terms):
    return lax.psum(row_terms, "proto")


def normalizers(proto_square, embed_square, proto_entries, embed_entries):
    totals = lax.psum((proto_square, embed_square), ("batch", "proto"))
    proto_factor = lax.rsqrt(totals[0] / proto_entries + NORM_EPS)
    embed_factor = lax.rsqrt(totals[1] / embed_entries + NORM_EPS)
    return (proto_factor, embed_factor)


def body(slow_embed, fast_embed, prototypes):
    clip_dev = slow_embed.shape[0]
    proto_dev = prototypes.shape[0]
    feat_width = prototypes.shape[1]
    batch_count = lax.axis_size("batch")
    proto_count = lax.axis_size("proto")
    clips_all = clip_dev * batch_count
    protos_all = proto_dev * proto_count
    proto_entries = float(protos_all * feat_width)
    embed_entries = float(2 * clips_all * feat_width)
    raw_views = jnp.stack([slow_embed, fast_embed]).astype(jnp.float32)
    unit_vec, lengths = normalize(raw_views)
    unit_b = unit_vec.astype(jnp.bfloat16)
    proto_unit, proto_len = normalize(prototypes)
    proto_b = proto_unit.astype(jnp.bfloat16)
    scores = jnp.einsum("vbd,kd->vbk", unit_b, proto_b, preferred_element_type=jnp.float32)
    code_table = jnp.exp(scores / CODE_EPS)
    soft_exp = jnp.exp(scores / TEMPER)
    denom_terms = jnp.sum(soft_exp, axis=2)
    denominator = lax.psum(denom_terms, "proto")
    clip_scale = jnp.ones((2, clip_dev), jnp.float32)
    for iteration in range(ITERS):
        col_total = lax.psum(jnp.sum(code_table * clip_scale[:, :, None], axis=1), "batch")
        proto_scale = 1.0 / (protos_all * col_total)
        row_terms = jnp.sum(code_table * proto_scale[:, None, :], axis=2)
        if iteration == 0:
            clip_total = row_total(row_terms)
        else:
            clip_total = row_total(row_terms)
        clip_scale = 1.0 / (clips_all * clip_total)
    codes = code_table * proto_scale[:, None, :] / clip_total[:, :, None]
    probs = soft_exp / denominator[:, :, None]
    score_grad = (jnp.stack([probs[0] - codes[1], probs[1] - codes[0]]) / TEMPER).astype(
        jnp.bfloat16
    )
    proto_terms = jnp.einsum("vbk,vbd->kd", score_grad, unit_b, preferred_element_type=jnp.float32)
    grad_proto_unit = lax.psum(proto_terms, "batch")
    embed_terms = jnp.einsum("vbk,kd->vbd", score_grad, proto_b, preferred_element_type=jnp.float32)
    grad_unit = lax.psum(embed_terms, "proto")
    grad_proto = project_back(grad_proto_unit, proto_unit, proto_len)
    grad_embed = project_back(grad_unit, unit_vec, lengths)
    proto_factor, embed_factor = normalizers(
        jnp.sum(grad_proto * grad_proto) / batch_count,
        jnp.sum(grad_embed * grad_embed) / proto_count,
        proto_entries,
        embed_entries,
    )
    proto_grad = grad_proto * proto_factor
    slow_grad = grad_embed[0] * embed_factor
    fast_grad = grad_embed[1] * embed_factor
    return (proto_grad, slow_grad, fast_grad)


def solution(mesh):
    placed = (P("batch", None), P("batch", None), P("proto", None))
    return jax.shard_map(
        body,
        mesh=mesh,
        in_specs=placed,
        out_specs=(P("proto", None), P("batch", None), P("batch", None)),
        check_vma=False,
    )
```

profile of v0, /device:TPU:1, one launch (start us, length us, event | category | flops | bytes accessed | tf_op | source)
XLA Modules:
  0.0 716.6 jit_solution(129335976540485152)
XLA Ops:
  7.2 0.0 all-reduce.5.cloned.1.call-start
  7.2 1.6 fusion.5
  8.8 1.9 multiply_reduce_fusion.9
  10.7 9.2 %fusion.4 = (f32[2,2048]{1,0:T(2,128)S(1)}, f32[2,1024,2048]{2,1,0:T(8,128)}) fusion(f32[2048,256]{1,0:T(8,128)} %param.5, f32[2048]{0:T(1024)S(1)} %add_sqrt_fusion, f32[2,1024]{1,0:T(2,128)S(1)} %add_sqrt_fusion.1, bf16[1,1024,256]{2,1,0:T(8,128)(2,1)} %bitcast.16, bf16[1,1024,256]{2,1,0:T(8,128)(2,1)} %bitcast.20), kind=kOutput, calls=%fused_computation.15 | convolution fusion | flops 2159013888 | bytes 19955712 | tf_op jit(solution)/shard_map/vbd,kd->vbk/dot_general | solution.py:48
  20.0 48.8 %psum.78 = f32[2,2048]{1,0:T(2,128)S(1)} all-reduce(f32[2,2048]{1,0:T(2,128)S(1)} %get-tuple-element.17), channel_id=1, replica_groups=mesh['batch'=16,'proto'=16] {'batch'}, use_global_device_ids=true, to_apply=%region_5.0 | all-reduce | flops 4096 | bytes 32768 | tf_op jit(solution)/shard_map/psum | solution.py:55
  68.8 9.0 %fusion.3 = (f32[2,1024]{1,0:T(2,128)S(1)}, f32[2,1024]{1,0:T(2,128)S(1)}) fusion(f32[2,1024,2048]{2,1,0:T(8,128)} %get-tuple-element.18, f32[2,2048]{1,0:T(2,128)S(1)} %multiply_divide_fusion.3), kind=kLoop, calls=%fused_computation.12 | loop fusion | flops 20967424 | bytes 16809984 | tf_op jit(solution)/shard_map/reduce_sum | solution.py:51
  77.8 34.0 %psum.79 = f32[2,1024]{1,0:T(2,128)S(1)} all-reduce(f32[2,1024]{1,0:T(2,128)S(1)} %get-tuple-element.4), channel_id=1, replica_groups=mesh['batch'=16,'proto'=16] {'proto'}, use_global_device_ids=true, to_apply=%region_7.0 | all-reduce | flops 2048 | bytes 16384 | tf_op jit(solution)/shard_map/psum | solution.py:23
  111.8 7.4 %multiply_reduce_fusion.2 = f32[2,2048]{1,0:T(2,128)S(1)} fusion(f32[2,1024]{1,0:T(2,128)S(1)} %multiply_divide_fusion.5, f32[2,1024,2048]{2,1,0:T(8,128)} %get-tuple-element.18), kind=kLoop, calls=%fused_computation.5 | loop fusion | flops 12578816 | bytes 16801792 | tf_op jit(solution)/shard_map/reduce_sum | solution.py:55
  119.1 52.9 %psum.80 = f32[2,2048]{1,0:T(2,128)S(1)} all-reduce(f32[2,2048]{1,0:T(2,128)S(1)} %multiply_reduce_fusion.2), channel_id=1, replica_groups=mesh['batch'=16,'proto'=16] {'batch'}, use_global_device_ids=true, to_apply=%region_9.0 | all-reduce | flops 4096 | bytes 32768 | tf_op jit(solution)/shard_map/psum | solution.py:55
  172.0 8.6 %multiply_reduce_fusion.1 = f32[2,1024]{1,0:T(2,128)S(1)} fusion(f32[2,2048]{1,0:T(2,128)S(1)} %multiply_divide_fusion.2, f32[2,1024,2048]{2,1,0:T(8,128)} %get-tuple-element.18), kind=kLoop, calls=%fused_computation.4 | loop fusion | flops 12580864 | bytes 16801792 | tf_op jit(solution)/shard_map/reduce_sum | solution.py:57
  180.6 29.0 %psum.81 = f32[2,1024]{1,0:T(2,128)S(1)} all-reduce(f32[2,1024]{1,0:T(2,128)S(1)} %multiply_reduce_fusion.1), channel_id=1, replica_groups=mesh['batch'=16,'proto'=16] {'proto'}, use_global_device_ids=true, to_apply=%region_11.0 | all-reduce | flops 2048 | bytes 16384 | tf_op jit(solution)/shard_map/psum | solution.py:23
  209.7 7.4 %multiply_reduce_fusion = f32[2,2048]{1,0:T(2,128)S(1)} fusion(f32[2,1024]{1,0:T(2,128)S(1)} %multiply_divide_fusion.4, f32[2,1024,2048]{2,1,0:T(8,128)} %get-tuple-element.18), kind=kLoop, calls=%fused_computation.3 | loop fusion | flops 12578816 | bytes 16801792 | tf_op jit(solution)/shard_map/reduce_sum | solution.py:55
  217.0 52.8 %psum.82 = f32[2,2048]{1,0:T(2,128)S(1)} all-reduce(f32[2,2048]{1,0:T(2,128)S(1)} %multiply_reduce_fusion), channel_id=1, replica_groups=mesh['batch'=16,'proto'=16] {'batch'}, use_global_device_ids=true, to_apply=%region_13.0 | all-reduce | flops 4096 | bytes 32768 | tf_op jit(solution)/shard_map/psum | solution.py:55
  269.9 8.6 %multiply_reduce_fusion.4 = f32[2,1024]{1,0:T(2,128)S(1)} fusion(f32[2,2048]{1,0:T(2,128)S(1)} %multiply_divide_fusion.1, f32[2,1024,2048]{2,1,0:T(8,128)} %get-tuple-element.18), kind=kLoop, calls=%fused_computation.10 | loop fusion | flops 12580864 | bytes 16801792 | tf_op jit(solution)/shard_map/reduce_sum | solution.py:57
  278.5 57.5 %all-reduce.1 = (f32[2,1024]{1,0:T(2,128)S(1)}, f32[2,1024]{1,0:T(2,128)S(1)}) all-reduce(f32[2,1024]{1,0:T(2,128)S(1)} %multiply_reduce_fusion.4, f32[2,1024]{1,0:T(2,128)S(1)} %get-tuple-element.3), channel_id=1, replica_groups=mesh['batch'=16,'proto'=16] {'proto'}, use_global_device_ids=true, to_apply=%region_15.0 | all-reduce | flops 4096 | bytes 32768 | tf_op jit(solution)/shard_map/psum | solution.py:23
  336.0 18.3 %fusion.2 = (f32[2,1024,2048]{2,1,0:T(8,128)}, f32[2,1024,2048]{2,1,0:T(8,128)}) fusion(f32[2,1024,2048]{2,1,0:T(8,128)} %get-tuple-element.18, f32[2,1024]{1,0:T(2,128)S(1)} %get-tuple-element.8, f32[2,1024]{1,0:T(2,128)S(1)} %get-tuple-element.7, f32[2,2048]{1,0:T(2,128)S(1)} %multiply_divide_fusion.1), kind=kLoop, calls=%fused_computation.11 | loop fusion | flops 20971520 | bytes 50364416 | tf_op jit(solution)/shard_map/div | solution.py:64
  354.3 0.0 copy-start.2
  354.3 0.0 copy-start.3
  354.3 19.2 %slice_subtract_fusion.1 = (f32[1,1024,2048]{2,1,0:T(8,128)}, f32[1,1024,2048]{2,1,0:T(8,128)}) fusion(f32[2,1024,2048]{2,1,0:T(8,128)} %get-tuple-element.14, f32[2,1024,2048]{2,1,0:T(8,128)} %get-tuple-element.13), kind=kLoop, calls=%fused_computation.14 | loop fusion | flops 4194304 | bytes 50331648 | tf_op jit(solution)/shard_map/sub | solution.py:65
  373.5 0.0 copy-done.2
  373.5 0.0 copy-done.3
  373.5 0.0 copy-start
  373.5 8.8 %convolution_bitcast_fusion = f32[2048,256]{1,0:T(8,128)} fusion(f32[1,1024,2048]{2,1,0:T(8,128)} %get-tuple-element.12, f32[1,1024,2048]{2,1,0:T(8,128)} %get-tuple-element.11, f32[2,1024]{1,0:T(2,128)S(1)} %add_sqrt_fusion.1, bf16[1,1024,256]{2,1,0:T(8,128)(2,1)S(1)} %bitcast.17, bf16[1,1024,256]{2,1,0:T(8,128)(2,1)S(1)} %bitcast.21), kind=kOutput, calls=%fused_computation.16 | convolution fusion | flops 2162163712 | bytes 19931136 | tf_op jit(solution)/shard_map/vbk,vbd->kd/dot_general | solution.py:68
  382.3 0.0 all-reduce.5.cloned.1.call-update
  382.3 0.3 all-reduce.7.cloned.1.call-start
  382.6 0.0 copy-done
  382.6 8.5 %fusion.11 = f32[2,1024,256]{2,1,0:T(8,128)} fusion(f32[1,1024,2048]{2,1,0:T(8,128)} %get-tuple-element.12, f32[1,1024,2048]{2,1,0:T(8,128)} %get-tuple-element.11, f32[2048,256]{1,0:T(8,128)S(1)} %copy-done, f32[2048]{0:T(1024)S(1)} %add_sqrt_fusion), kind=kOutput, calls=%fused_computation.33 | convolution fusion | flops 2161115136 | bytes 20979712 | tf_op jit(solution)/shard_map/vbk,kd->vbd/dot_general | solution.py:70
  391.1 0.0 all-reduce.7.cloned.1.call-update
  391.2 116.1 %all-reduce.5.cloned.1.call-done = f32[2048,256]{1,0:T(8,128)} async-done(((f32[2048,256]{1,0:T(8,128)}), f32[2048,256]{1,0:T(8,128)}) %all-reduce.5.cloned.1.call-update) | async-done | bytes 2097168 | tf_op jit(solution)/shard_map/psum | solution.py:69
  507.3 2.2 multiply_reduce_fusion.8
  509.5 3.6 multiply_reduce_fusion.7
  513.8 0.0 copy-start.1
  513.8 97.2 %all-reduce.7.cloned.1.call-done = f32[2,1024,256]{2,1,0:T(8,128)} async-done(((f32[2,1024,256]{2,1,0:T(8,128)}), f32[2,1024,256]{2,1,0:T(8,128)}) %all-reduce.7.cloned.1.call-update) | async-done | bytes 2097168 | tf_op jit(solution)/shard_map/psum | solution.py:71
  611.0 15.5 %multiply_reduce_fusion.5 = (f32[]{:T(128)}, f32[2,1024,256]{2,1,0:T(8,128)}) fusion(f32[2,1024,256]{2,1,0:T(8,128)} %all-reduce.7.cloned.1.call-done, f32[2,1024]{1,0:T(2,128)S(1)} %add_sqrt_fusion.1, bf16[1,1024,256]{2,1,0:T(8,128)(2,1)S(1)} %bitcast.18, bf16[1,1024,256]{2,1,0:T(8,128)(2,1)S(1)} %bitcast.22), kind=kOutput, calls=%fused_computation.20 | output fusion | flops 7342334 | bytes 5251076 | tf_op jit(solution)/shard_map/mul | solution.py:19
  627.1 76.8 %all-reduce = (f32[]{:T(128)}, f32[]{:T(128)}) all-reduce(f32[]{:T(128)S(6)} %div.101, f32[]{:T(128)S(6)} %div.104), channel_id=1, replica_groups=mesh['batch'=16,'proto'=16] {'batch','proto'}, use_global_device_ids=true, to_apply=%region_19.0 | all-reduce | flops 2 | bytes 16 | tf_op jit(solution)/shard_map/psum | solution.py:27
  705.3 0.0 copy-done.1
  705.3 1.5 broadcast_multiply_fusion
  706.8 3.0 fusion.9
  (7 shorter events, 0.1 us)
Async XLA Ops:
  7.2 500.1 %all-reduce.5.cloned.1.call-start = ((), (), s32[]{:S(2)}) async-start(), calls=%async_computation | async-start | bytes 4194304 | tf_op jit(solution)/shard_map/psum | solution.py:69
  354.3 19.2 %copy-start.2 = (bf16[1024,256]{1,0:T(8,128)(2,1)S(1)}, bf16[1024,256]{1,0:T(8,128)(2,1)}, u32[]{:S(2)}) copy-start(bf16[1024,256]{1,0:T(8,128)(2,1)} %param.4) | copy-start | bytes 1572868
  354.3 19.2 %copy-start.3 = (bf16[1024,256]{1,0:T(8,128)(2,1)S(1)}, bf16[1024,256]{1,0:T(8,128)(2,1)}, u32[]{:S(2)}) copy-start(bf16[1024,256]{1,0:T(8,128)(2,1)} %param.3) | copy-start | bytes 1572868
  373.5 9.1 %copy-start = (f32[2048,256]{1,0:T(8,128)S(1)}, f32[2048,256]{1,0:T(8,128)}, u32[]{:S(2)}) copy-start(f32[2048,256]{1,0:T(8,128)} %param.5) | copy-start | bytes 6291460
  382.3 228.7 %all-reduce.7.cloned.1.call-start = ((), (), s32[]{:S(2)}) async-start(), calls=%async_computation.1 | async-start | bytes 4194304 | tf_op jit(solution)/shard_map/psum | solution.py:71
  513.8 191.5 %copy-start.1 = (f32[2048,256]{1,0:T(8,128)S(1)}, f32[2048,256]{1,0:T(8,128)}, u32[]{:S(2)}) copy-start(f32[2048,256]{1,0:T(8,128)} %get-tuple-element.10) | copy-start | bytes 6291460
Sparse Core Ops, SparseCore 0:
  382.4 124.8 all-reduce.4
  510.6 100.3 all-reduce.6
where the time goes:
time: 717 us
  blocking collectives  352 us (49%)
  waiting for transfers between devices  213 us (30%)
  other arithmetic  108 us (15%)
  matrix products  26.5 us (4%)
  between operations  16.9 us (2%)
    psum x3, blocking collectives, body(): lax.psum(jnp.sum(code_table * clip_scale[:, :, None], axis=1), 'batch')  155 us
    psum x3, blocking collectives, row_total(): return lax.psum(row_terms, 'proto')  121 us
    psum x1, waiting for transfers between devices, body(): grad_proto_unit = lax.psum(proto_terms, 'batch')  116 us
    psum x1, waiting for transfers between devices, body(): grad_unit = lax.psum(embed_terms, 'proto')  97.2 us
    psum x1, blocking collectives, normalizers(): totals = lax.psum((proto_square, embed_square), ('batch', 'proto'))  76.8 us
    sub x1, other arithmetic, body(): probs[0] - codes[1]  19.2 us
    div x1, other arithmetic, body(): probs = soft_exp / denominator[:, :, None]  18.3 us
    reduce_sum x2, other arithmetic, body(): row_terms = jnp.sum(code_table * proto_scale[:, None, :], axis=2)  17.2 us
  transfers between devices with their start and end apart: 2, of which 2 were waited for; matrix products, arithmetic and copies ran while one was open for 2% of the time, Pallas kernels for 0%

commit v1 on v0

--- a/solution.py
+++ b/solution.py
@@ -7,6 +7,14 @@
 CODE_EPS = 0.05
 TEMPER = 0.1
 NORM_EPS = 1e-06
+
+
+def added_up(shard, axis):
+    size, acc = (lax.axis_size(axis), shard)
+    for stride in [1 << k for k in range(size.bit_length() - 1)]:
+        swap = [(i, i ^ stride) for i in range(size)]
+        acc = acc + lax.ppermute(acc, axis, swap)
+    return acc
 
 
 def normalize(raw_rows):
@@ -68,7 +76,7 @@
     proto_terms = jnp.einsum("vbk,vbd->kd", score_grad, unit_b, preferred_element_type=jnp.float32)
     grad_proto_unit = lax.psum(proto_terms, "batch")
     embed_terms = jnp.einsum("vbk,kd->vbd", score_grad, proto_b, preferred_element_type=jnp.float32)
-    grad_unit = lax.psum(embed_terms, "proto")
+    grad_unit = added_up(embed_terms, "proto")
     grad_proto = project_back(grad_proto_unit, proto_unit, proto_len)
     grad_embed = project_back(grad_unit, unit_vec, lengths)
     proto_factor, embed_factor = normalizers(

time: 717 us -> 749 us (1.045)
  waiting for transfers between devices: 213 us -> 243 us
  other arithmetic: 108 us -> 100 us
  starting transfers between devices: 0.3 us -> 7.97 us
    psum x1 -> x0, waiting for transfers between devices: 97.2 us -> none  [body(): grad_unit = lax.psum(embed_terms, 'proto')]
    ppermute x0 -> x4, waiting for transfers between devices: none -> 96.2 us  [added_up(): acc = acc + lax.ppermute(acc, axis, swap)]
    psum x1, waiting for transfers between devices: 116 us -> 147 us  [body(): grad_proto_unit = lax.psum(proto_terms, 'batch')]
    mul x1, other arithmetic: 15.5 us -> 6.62 us  [project_back(): return (grad_unit - unit_vec * along) / lengths]
    ppermute x0 -> x4, starting transfers between devices: none -> 7.93 us  [added_up(): acc = acc + lax.ppermute(acc, axis, swap)]
  transfers between devices with their start and end apart: 2 -> 5, of which waited for: 2 -> 4; matrix products, arithmetic and copies ran while one was open for 2% -> 1% of each run, Pallas kernels for 0% -> 0%
where the time goes in v1:
time: 749 us; the launch traced here: 748 us
  blocking collectives  353 us (47%)
  waiting for transfers between devices  243 us (32%)
  other arithmetic  100 us (13%)
  matrix products  20.7 us (3%)
  between operations  17.1 us (2%)
  starting transfers between devices  7.97 us (1%)
    psum x3, blocking collectives, body(): lax.psum(jnp.sum(code_table * clip_scale[:, :, None], axis=1), 'batch')  155 us
    psum x1, waiting for transfers between devices, body(): grad_proto_unit = lax.psum(proto_terms, 'batch')  147 us
    psum x3, blocking collectives, row_total(): return lax.psum(row_terms, 'proto')  121 us
    ppermute x4, waiting for transfers between devices, added_up(): acc = acc + lax.ppermute(acc, axis, swap)  96.2 us
    psum x1, blocking collectives, normalizers(): totals = lax.psum((proto_square, embed_square), ('batch', 'proto'))  77.9 us
    sub x1, other arithmetic, body(): probs[0] - codes[1]  19.2 us
    div x1, other arithmetic, body(): probs = soft_exp / denominator[:, :, None]  18.3 us
    reduce_sum x2, other arithmetic, body(): row_terms = jnp.sum(code_table * proto_scale[:, None, :], axis=2)  17.2 us
  transfers between devices with their start and end apart: 5, of which 4 were waited for; matrix products, arithmetic and copies ran while one was open for 1% of the time, Pallas kernels for 0%

profile of v1, /device:TPU:1, one launch (start us, length us, event | category | flops | bytes accessed | tf_op | source)
XLA Modules:
  0.0 748.4 jit_solution(7811103556797707655)
XLA Ops:
  7.2 0.0 all-reduce.4.cloned.1.call-start
  7.2 1.9 multiply_reduce_fusion.9
  9.2 1.2 copy.6
  10.4 1.2 copy.7
  11.7 0.2 fusion.5
  11.9 9.2 %fusion.4 = (f32[2,2048]{1,0:T(2,128)S(1)}, f32[2,1024,2048]{2,1,0:T(8,128)}) fusion(f32[2048,256]{1,0:T(8,128)} %param.5, f32[2048]{0:T(1024)S(1)} %add_sqrt_fusion, f32[2,1024]{1,0:T(2,128)S(1)} %add_sqrt_fusion.1, bf16[1,1024,256]{1,2,0:T(8,128)(2,1)S(1)} %bitcast.25, bf16[1,1024,256]{1,2,0:T(8,128)(2,1)S(1)} %bitcast.21), kind=kOutput, calls=%fused_computation.15 | convolution fusion | flops 2159013888 | bytes 19955712 | tf_op jit(solution)/shard_map/vbd,kd->vbk/dot_general | solution.py:56
  21.2 48.8 %psum.71 = f32[2,2048]{1,0:T(2,128)S(1)} all-reduce(f32[2,2048]{1,0:T(2,128)S(1)} %get-tuple-element.20), channel_id=1, replica_groups=mesh['batch'=16,'proto'=16] {'batch'}, use_global_device_ids=true, to_apply=%region_5.0 | all-reduce | flops 4096 | bytes 32768 | tf_op jit(solution)/shard_map/psum | solution.py:63
  70.0 9.0 %fusion.3 = (f32[2,1024]{1,0:T(2,128)S(1)}, f32[2,1024]{1,0:T(2,128)S(1)}) fusion(f32[2,1024,2048]{2,1,0:T(8,128)} %get-tuple-element.21, f32[2,2048]{1,0:T(2,128)S(1)} %multiply_divide_fusion.3), kind=kLoop, calls=%fused_computation.12 | loop fusion | flops 20967424 | bytes 16809984 | tf_op jit(solution)/shard_map/reduce_sum | solution.py:59
  79.0 34.0 %psum.72 = f32[2,1024]{1,0:T(2,128)S(1)} all-reduce(f32[2,1024]{1,0:T(2,128)S(1)} %get-tuple-element.7), channel_id=1, replica_groups=mesh['batch'=16,'proto'=16] {'proto'}, use_global_device_ids=true, to_apply=%region_7.0 | all-reduce | flops 2048 | bytes 16384 | tf_op jit(solution)/shard_map/psum | solution.py:31
  113.0 7.4 multiply_reduce_fusion.2
  120.3 52.9 %psum.73 = f32[2,2048]{1,0:T(2,128)S(1)} all-reduce(f32[2,2048]{1,0:T(2,128)S(1)} %multiply_reduce_fusion.2), channel_id=1, replica_groups=mesh['batch'=16,'proto'=16] {'batch'}, use_global_device_ids=true, to_apply=%region_9.0 | all-reduce | flops 4096 | bytes 32768 | tf_op jit(solution)/shard_map/psum | solution.py:63
  173.3 8.6 %multiply_reduce_fusion.1 = f32[2,1024]{1,0:T(2,128)S(1)} fusion(f32[2,2048]{1,0:T(2,128)S(1)} %multiply_divide_fusion.2, f32[2,1024,2048]{2,1,0:T(8,128)} %get-tuple-element.21), kind=kLoop, calls=%fused_computation.4 | loop fusion | flops 12580864 | bytes 16801792 | tf_op jit(solution)/shard_map/reduce_sum | solution.py:65
  181.9 29.0 %psum.74 = f32[2,1024]{1,0:T(2,128)S(1)} all-reduce(f32[2,1024]{1,0:T(2,128)S(1)} %multiply_reduce_fusion.1), channel_id=1, replica_groups=mesh['batch'=16,'proto'=16] {'proto'}, use_global_device_ids=true, to_apply=%region_11.0 | all-reduce | flops 2048 | bytes 16384 | tf_op jit(solution)/shard_map/psum | solution.py:31
  210.9 7.4 multiply_reduce_fusion
  218.3 52.8 %psum.75 = f32[2,2048]{1,0:T(2,128)S(1)} all-reduce(f32[2,2048]{1,0:T(2,128)S(1)} %multiply_reduce_fusion), channel_id=1, replica_groups=mesh['batch'=16,'proto'=16] {'batch'}, use_global_device_ids=true, to_apply=%region_13.0 | all-reduce | flops 4096 | bytes 32768 | tf_op jit(solution)/shard_map/psum | solution.py:63
  271.1 8.6 %multiply_reduce_fusion.4 = f32[2,1024]{1,0:T(2,128)S(1)} fusion(f32[2,2048]{1,0:T(2,128)S(1)} %multiply_divide_fusion.1, f32[2,1024,2048]{2,1,0:T(8,128)} %get-tuple-element.21), kind=kLoop, calls=%fused_computation.10 | loop fusion | flops 12580864 | bytes 16801792 | tf_op jit(solution)/shard_map/reduce_sum | solution.py:65
  279.7 57.5 %all-reduce.1 = (f32[2,1024]{1,0:T(2,128)S(1)}, f32[2,1024]{1,0:T(2,128)S(1)}) all-reduce(f32[2,1024]{1,0:T(2,128)S(1)} %multiply_reduce_fusion.4, f32[2,1024]{1,0:T(2,128)S(1)} %get-tuple-element.6), channel_id=1, replica_groups=mesh['batch'=16,'proto'=16] {'proto'}, use_global_device_ids=true, to_apply=%region_15.0 | all-reduce | flops 4096 | bytes 32768 | tf_op jit(solution)/shard_map/psum | solution.py:31
  337.2 18.3 %fusion.2 = (f32[2,1024,2048]{2,1,0:T(8,128)}, f32[2,1024,2048]{2,1,0:T(8,128)}) fusion(f32[2,1024,2048]{2,1,0:T(8,128)} %get-tuple-element.21, f32[2,1024]{1,0:T(2,128)S(1)} %get-tuple-element.11, f32[2,1024]{1,0:T(2,128)S(1)} %get-tuple-element.10, f32[2,2048]{1,0:T(2,128)S(1)} %multiply_divide_fusion.1), kind=kLoop, calls=%fused_computation.11 | loop fusion | flops 20971520 | bytes 50364416 | tf_op jit(solution)/shard_map/div | solution.py:72
  355.5 19.2 %slice_subtract_fusion.1 = (f32[1,1024,2048]{2,1,0:T(8,128)}, f32[1,1024,2048]{2,1,0:T(8,128)}) fusion(f32[2,1024,2048]{2,1,0:T(8,128)} %get-tuple-element.17, f32[2,1024,2048]{2,1,0:T(8,128)} %get-tuple-element.16), kind=kLoop, calls=%fused_computation.14 | loop fusion | flops 4194304 | bytes 50331648 | tf_op jit(solution)/shard_map/sub | solution.py:73
  374.7 0.0 copy-done
  374.7 0.0 slice-start.3
  374.8 7.4 fusion.11
  382.2 0.0 slice-start
  382.2 0.1 collective-permute-start
  382.3 29.8 %collective-permute-done = f32[2,1024,256]{1,2,0:T(8,128)S(1)} collective-permute-done((f32[2,1024,256]{1,2,0:T(8,128)S(1)}, f32[2,1024,256]{1,2,0:T(8,128)S(1)}, u32[]{:S(2)}, u32[]{:S(2)}) %collective-permute-start) | collective-permute-done | bytes 2097184 | tf_op jit(solution)/shard_map/ppermute | solution.py:16
  412.0 0.5 add.65
  412.5 0.0 slice-start.1
  412.5 0.1 collective-permute-start.1
  412.6 40.4 %collective-permute-done.1 = f32[2,1024,256]{1,2,0:T(8,128)S(1)} collective-permute-done((f32[2,1024,256]{1,2,0:T(8,128)S(1)}, f32[2,1024,256]{1,2,0:T(8,128)S(1)}, u32[]{:S(2)}, u32[]{:S(2)}) %collective-permute-start.1) | collective-permute-done | bytes 2097184 | tf_op jit(solution)/shard_map/ppermute | solution.py:16
  453.0 0.4 add.66
  453.5 0.1 collective-permute-start.2
  453.6 26.0 %collective-permute-done.2 = f32[2,1024,256]{1,2,0:T(8,128)S(1)} collective-permute-done((f32[2,1024,256]{1,2,0:T(8,128)S(1)}, f32[2,1024,256]{1,2,0:T(8,128)S(1)}, u32[]{:S(2)}, u32[]{:S(2)}) %collective-permute-start.2) | collective-permute-done | bytes 2097184 | tf_op jit(solution)/shard_map/ppermute | solution.py:16
  479.6 1.7 add.67
  481.4 7.7 %collective-permute-start.3 = (f32[2,1024,256]{1,2,0:T(8,128)}, f32[2,1024,256]{1,2,0:T(8,128)}, u32[]{:S(2)}, u32[]{:S(2)}) collective-permute-start(f32[2,1024,256]{1,2,0:T(8,128)} %add.67), channel_id=1, source_target_pairs={{0,8},{1,9},{2,10},{3,11},{4,12},{5,13},{6,14},{7,15},{8,0},{9,1},... | collective-permute-start | bytes 6291464 | tf_op jit(solution)/shard_map/ppermute | solution.py:16
  489.0 0.0 slice-done.2
  489.0 0.0 slice-done.3
  489.0 4.0 convolution_bitcast_fusion
  493.1 0.0 all-reduce.4.cloned.1.call-update
  493.1 147.2 %all-reduce.4.cloned.1.call-done = f32[2048,256]{1,0:T(8,128)} async-done(((f32[2048,256]{1,0:T(8,128)}), f32[2048,256]{1,0:T(8,128)}) %all-reduce.4.cloned.1.call-update) | async-done | bytes 2097168 | tf_op jit(solution)/shard_map/psum | solution.py:77
  640.3 2.2 multiply_reduce_fusion.8
  642.5 3.6 multiply_reduce_fusion.7
  646.8 0.0 collective-permute-done.3
  646.8 6.6 multiply_reduce_fusion.5
  654.2 77.9 %all-reduce = (f32[]{:T(128)}, f32[]{:T(128)}) all-reduce(f32[]{:T(128)S(6)} %div.101, f32[]{:T(128)S(6)} %div.104), channel_id=1, replica_groups=mesh['batch'=16,'proto'=16] {'batch','proto'}, use_global_device_ids=true, to_apply=%region_19.0 | all-reduce | flops 2 | bytes 16 | tf_op jit(solution)/shard_map/psum | solution.py:35
  733.5 2.7 fusion.9
  736.3 2.5 copy.13
  738.8 1.3 copy.12
  740.1 1.5 broadcast_multiply_fusion
  (15 shorter events, 0.1 us)
Async XLA Ops:
  7.2 633.1 %all-reduce.4.cloned.1.call-start = ((), (), s32[]{:S(2)}) async-start(), calls=%async_computation | async-start | bytes 4194304 | tf_op jit(solution)/shard_map/psum | solution.py:77
  355.5 19.3 %copy-start = (f32[2048,256]{1,0:T(8,128)S(1)}, f32[2048,256]{1,0:T(8,128)}, u32[]{:S(2)}) copy-start(f32[2048,256]{1,0:T(8,128)} %param.5) | copy-start | bytes 6291460
  374.7 114.3 %slice-start.2 = ((s8[8388608]{0:T(1024)(128)(4,1)}), s8[4194304]{0:T(1024)(128)(4,1)S(1)}, s32[]{:S(2)}) async-start(s8[8388608]{0:T(1024)(128)(4,1)} %bitcast.18), calls=%async_computation.3 | async-start | bytes 8388608
  374.7 114.3 %slice-start.3 = ((s8[8388608]{0:T(1024)(128)(4,1)}), s8[4194304]{0:T(1024)(128)(4,1)S(1)}, s32[]{:S(2)}) async-start(s8[8388608]{0:T(1024)(128)(4,1)} %bitcast.18), calls=%async_computation.4 | async-start | bytes 8388608
  382.2 106.9 %slice-start = ((s8[8388608]{0:T(1024)(128)(4,1)}), s8[4194304]{0:T(1024)(128)(4,1)S(1)}, s32[]{:S(2)}) async-start(s8[8388608]{0:T(1024)(128)(4,1)} %bitcast.16), calls=%async_computation.1 | async-start | bytes 8388608
  382.2 29.9 %collective-permute-start = (f32[2,1024,256]{1,2,0:T(8,128)S(1)}, f32[2,1024,256]{1,2,0:T(8,128)S(1)}, u32[]{:S(2)}, u32[]{:S(2)}) collective-permute-start(f32[2,1024,256]{1,2,0:T(8,128)S(1)} %fusion.11), channel_id=1, source_target_pairs={{0,1},{1,0},{2,3},{3,2},{4,5},{5,4},{6,7},{7,6},{8,9},{9,8},{10,11... | collective-permute-start | bytes 6291464 | tf_op jit(solution)/shard_map/ppermute | solution.py:16
  412.5 76.5 %slice-start.1 = ((s8[8388608]{0:T(1024)(128)(4,1)}), s8[4194304]{0:T(1024)(128)(4,1)S(1)}, s32[]{:S(2)}) async-start(s8[8388608]{0:T(1024)(128)(4,1)} %bitcast.16), calls=%async_computation.2 | async-start | bytes 8388608
  412.5 40.5 %collective-permute-start.1 = (f32[2,1024,256]{1,2,0:T(8,128)S(1)}, f32[2,1024,256]{1,2,0:T(8,128)S(1)}, u32[]{:S(2)}, u32[]{:S(2)}) collective-permute-start(f32[2,1024,256]{1,2,0:T(8,128)S(1)} %add.65), channel_id=1, source_target_pairs={{0,2},{1,3},{2,0},{3,1},{4,6},{5,7},{6,4},{7,5},{8,10},{9,11},{10,... | collective-permute-start | bytes 6291464 | tf_op jit(solution)/shard_map/ppermute | solution.py:16
  453.5 26.1 %collective-permute-start.2 = (f32[2,1024,256]{1,2,0:T(8,128)S(1)}, f32[2,1024,256]{1,2,0:T(8,128)S(1)}, u32[]{:S(2)}, u32[]{:S(2)}) collective-permute-start(f32[2,1024,256]{1,2,0:T(8,128)S(1)} %add.66), channel_id=1, source_target_pairs={{0,4},{1,5},{2,6},{3,7},{4,0},{5,1},{6,2},{7,3},{8,12},{9,13},{10,... | collective-permute-start | bytes 6291464 | tf_op jit(solution)/shard_map/ppermute | solution.py:16
  481.4 165.4 %collective-permute-start.3 = (f32[2,1024,256]{1,2,0:T(8,128)}, f32[2,1024,256]{1,2,0:T(8,128)}, u32[]{:S(2)}, u32[]{:S(2)}) collective-permute-start(f32[2,1024,256]{1,2,0:T(8,128)} %add.67), channel_id=1, source_target_pairs={{0,8},{1,9},{2,10},{3,11},{4,12},{5,13},{6,14},{7,15},{8,0},{9,1},... | collective-permute-start | bytes 6291464 | tf_op jit(solution)/shard_map/ppermute | solution.py:16
  653.4 86.7 %copy-start.1 = (f32[2048,256]{1,0:T(8,128)S(1)}, f32[2048,256]{1,0:T(8,128)}, u32[]{:S(2)}) copy-start(f32[2048,256]{1,0:T(8,128)} %get-tuple-element.13) | copy-start | bytes 6291460
Sparse Core Ops, SparseCore 0:
  493.2 146.9 all-reduce.3
